TPU v7x, 32 devices: a whole 2x2x4 slice. The times are simulated.
32 devices in a mesh: rep: 4 (over y, x), tp: 8 (over z, core).
Axes of the slice: x: 2, y: 2, z: 4, core: 2. Of those that a mesh axis runs over, the one named last changes fastest.
Arguments:
- deltas: bfloat16 [4, 3, 4096, 8192], P('rep', None, 'tp'), may hold values from -2600 to 2600
- staleness: int32 [4], P('rep'), may hold values from 0 to 2
Outputs:
- update: bfloat16 [4096, 8192], P('tp')
All inputs are finite; a program needn't handle non-finite values.
Results may differ from a plain program's by a relative error of at most 0.028.
Values may be sent and summed in bfloat16 or wider, within the bound.
A program may use at most 128 MiB of HBM per device.

v0:
```python
import jax
import jax.numpy as jnp
from jax import lax
from jax.sharding import PartitionSpec as P

TILE = 512
NS_ITERS = 5


damping = 0.001


def multiply(left_side, right_side):
    return jnp.einsum("xij,xjk->xik", left_side, right_side, precision=lax.Precision.HIGHEST)


def inverse_roots(stat_stack):
    identity = jnp.eye(TILE, dtype=jnp.float32)
    frob_norm = jnp.sqrt(jnp.sum(stat_stack * stat_stack, axis=(1, 2), keepdims=True))
    current = stat_stack / frob_norm
    iterate = jnp.broadcast_to(identity, stat_stack.shape)
    for step in range(NS_ITERS):
        factor = (5.0 * identity - current) * 0.25
        iterate = multiply(iterate, factor)
        if step + 1 < NS_ITERS:
            square = multiply(factor, factor)
            fourth = multiply(square, square)
            current = multiply(fourth, current)
    return (iterate * frob_norm ** (-0.25)).astype(jnp.bfloat16)


def to_grid(strip_rows, tile):
    return strip_rows.reshape(
        strip_rows.shape[0] // tile, tile, strip_rows.shape[1] // tile, tile
    ).transpose(0, 2, 1, 3)


def to_strip(tile_grid):
    grid_rows, grid_cols, tile, _ = tile_grid.shape
    return tile_grid.transpose(0, 2, 1, 3).reshape(grid_rows * tile, grid_cols * tile)


def precondition(root_grid, mean_tiles):
    half_product = jnp.einsum(
        "abij,abjk->abik", root_grid[:, :, 0], mean_tiles, preferred_element_type=jnp.float32
    ).astype(jnp.bfloat16)
    return jnp.einsum(
        "abij,abjk->abik", half_product, root_grid[:, :, 1], preferred_element_type=jnp.float32
    ).astype(jnp.bfloat16)


def local(deltas, staleness):
    replicas = lax.axis_size("rep")
    picked = lax.dynamic_index_in_dim(deltas[0], staleness[0], 0, keepdims=False)
    column_strip = lax.all_to_all(picked, "tp", split_axis=1, concat_axis=0, tiled=True)
    grid_rows = column_strip.shape[0] // TILE
    grid_cols = column_strip.shape[1] // TILE
    own_rows = grid_rows // replicas
    tile_set = to_grid(column_strip, TILE)
    left_gram = jnp.einsum(
        "abik,abjk->abij", tile_set, tile_set, preferred_element_type=jnp.float32
    )
    right_gram = jnp.einsum(
        "abki,abkj->abij", tile_set, tile_set, preferred_element_type=jnp.float32
    )
    gram_stack = jnp.stack([left_gram, right_gram], axis=2).reshape(
        grid_rows * grid_cols * 2, TILE, TILE
    )
    gram_sums, strip_sum = (
        lax.psum_scatter(
            gram_stack.astype(jnp.bfloat16), "rep", scatter_dimension=0, tiled=True
        ).astype(jnp.float32),
        lax.psum_scatter(
            column_strip.astype(jnp.float32).astype(jnp.bfloat16),
            "rep",
            scatter_dimension=0,
            tiled=True,
        ).astype(jnp.float32),
    )
    mean_part = (strip_sum / replicas).astype(jnp.bfloat16)
    identity = jnp.eye(TILE, dtype=jnp.float32)
    root_stack = inverse_roots(gram_sums / (replicas * TILE) + damping * identity)
    local_tiles = precondition(
        root_stack.reshape(own_rows, grid_cols, 2, TILE, TILE), to_grid(mean_part, TILE)
    )
    gathered = lax.all_gather(to_strip(local_tiles), "rep", axis=0, tiled=True)
    return lax.all_to_all(gathered, "tp", split_axis=0, concat_axis=1, tiled=True)


def solution(mesh):
    return jax.shard_map(
        local,
        mesh=mesh,
        in_specs=(P("rep", None, "tp", None), P("rep")),
        out_specs=P("tp", None),
        check_vma=False,
    )
```

profile of v0, /device:TPU:0, one launch (start us, length us, event | category | flops | bytes accessed | tf_op | source)
XLA Modules:
  0.0 1114.3 jit_solution(13952896521547234226)
XLA Ops:
  26.9 190.5 %all_to_all.38 = bf16[512,8,1024]{0,2,1:T(8,128)(2,1)} all-to-all(bf16[512,8,1024]{0,2,1:T(8,128)(2,1)} %bitcast.82), channel_id=1, replica_groups=mesh['rep'=4,'tp'=8] {'tp'}, dimensions={1} | all-to-all | bytes 16777216 | tf_op jit(solution)/shard_map/all_to_all | solution.py:55
  228.9 12.4 %copy.13 = bf16[8,512,2,512]{3,1,2,0:T(8,128)(2,1)} copy(bf16[8,512,2,512]{1,3,2,0:T(8,128)(2,1)} %bitcast.78) | data formatting | bytes 16777216 | tf_op jit(solution)/shard_map/reshape | solution.py:33
  253.1 14.0 %convert_bitcast_fusion = bf16[8,2,1,512,512]{4,3,1,0,2:T(8,128)(2,1)} fusion(bf16[8,2,512,512]{2,3,1,0:T(8,128)(2,1)} %bitcast.79, bf16[8,512,2,512]{3,1,2,0:T(8,128)(2,1)} %copy.13), kind=kOutput, calls=%fused_computation.16 | convolution fusion | flops 4299161600 | bytes 25165824 | tf_op jit(solution)/shard_map/abki,abkj->abij/dot_general | solution.py:63
  285.1 29.8 %reduce-scatter.5.cloned.1.call-done = bf16[1024,1024]{1,0:T(8,128)(2,1)} async-done(((bf16[4096,1024]{1,0:T(8,128)(2,1)}), bf16[1024,1024]{1,0:T(8,128)(2,1)}) %reduce-scatter.5.cloned.1.call-update) | async-done | bytes 2097168 | tf_op jit(solution)/shard_map/reduce_scatter | solution.py:73
  319.7 152.0 %reduce-scatter.3.cloned.1.call-done = bf16[8,512,512]{2,1,0:T(8,128)(2,1)} async-done(((bf16[32,512,512]{2,1,0:T(8,128)(2,1)}), bf16[8,512,512]{2,1,0:T(8,128)(2,1)}) %reduce-scatter.3.cloned.1.call-update) | async-done | bytes 4194320 | tf_op jit(solution)/shard_map/reduce_scatter | solution.py:70
  475.7 21.6 %fusion.8 = f32[8,512,512]{2,1,0:T(8,128)S(1)} fusion(f32[512,512]{1,0:T(8,128)S(1)} %get-tuple-element.8, bf16[8,512,512]{2,1,0:T(8,128)(2,1)} %reduce-scatter.3.cloned.1.call-done, f32[8]{0:T(128)S(1)} %get-tuple-element.5, f32[512,512]{1,0:T(8,128)} %get-tuple-element.7), kind=kOutput, calls=%fused_computation.18 | convolution fusion | flops 12897484800 | bytes 14680096 | tf_op jit(solution)/shard_map/xij,xjk->xik/dot_general | solution.py:14
  497.3 16.4 %fusion.69 = f32[8,512,512]{2,1,0:T(8,128)} fusion(f32[8,512,512]{2,1,0:T(8,128)S(1)} %fusion.8), kind=kOutput, calls=%fused_computation.71 | convolution fusion | flops 12884901888 | bytes 16777216 | tf_op jit(solution)/shard_map/xij,xjk->xik/dot_general | solution.py:14
  513.7 18.2 %fusion.65 = f32[8,512,512]{2,1,0:T(8,128)S(1)} fusion(f32[8,512,512]{2,1,0:T(8,128)} %fusion.69, bf16[8,512,512]{2,1,0:T(8,128)(2,1)S(1)} %copy-done.2, f32[8]{0:T(128)S(1)} %get-tuple-element.5, f32[512,512]{1,0:T(8,128)S(1)} %copy-done.3), kind=kOutput, calls=%fused_computation.69 | convolution fusion | flops 12893290496 | bytes 22020128 | tf_op jit(solution)/shard_map/xij,xjk->xik/dot_general | solution.py:14
  531.9 17.3 %fusion.10 = f32[8,512,512]{2,1,0:T(8,128)} fusion(f32[8,512,512]{2,1,0:T(8,128)S(1)} %fusion.65, f32[512,512]{1,0:T(8,128)S(1)} %get-tuple-element.8), kind=kOutput, calls=%fused_computation.20 | convolution fusion | flops 12889096192 | bytes 17825792 | tf_op jit(solution)/shard_map/xij,xjk->xik/dot_general | solution.py:14
  549.2 17.2 %fusion.9 = f32[8,512,512]{2,1,0:T(8,128)} fusion(f32[512,512]{1,0:T(8,128)S(1)} %get-tuple-element.8, f32[512,512]{1,0:T(8,128)S(1)} %copy-done.5, bf16[8,512,512]{2,1,0:T(8,128)(2,1)S(1)} %copy-done.2, f32[8]{0:T(128)S(1)} %get-tuple-element.5, f32[512,512]{1,0:T(8,128)S(1)} %copy-done.3), kind=kOutput, calls=%fused_computation.19 | convolution fusion | flops 12897484800 | bytes 15728672 | tf_op jit(solution)/shard_map/xij,xjk->xik/dot_general | solution.py:14
  566.4 17.6 %fusion.11 = f32[8,512,512]{2,1,0:T(8,128)} fusion(f32[8,512,512]{2,1,0:T(8,128)} %fusion.9, f32[8,512,512]{2,1,0:T(8,128)S(1)} %fusion.65, f32[512,512]{1,0:T(8,128)S(1)} %get-tuple-element.8), kind=kOutput, calls=%fused_computation.21 | convolution fusion | flops 12889096192 | bytes 26214400 | tf_op jit(solution)/shard_map/xij,xjk->xik/dot_general | solution.py:14
  584.0 21.9 %fusion.70 = f32[8,512,512]{2,1,0:T(8,128)} fusion(f32[8,512,512]{2,1,0:T(8,128)} %fusion.10), kind=kOutput, calls=%fused_computation.72 | convolution fusion | flops 12884901888 | bytes 16777216 | tf_op jit(solution)/shard_map/xij,xjk->xik/dot_general | solution.py:14
  605.9 16.4 %fusion.71 = f32[8,512,512]{2,1,0:T(8,128)S(1)} fusion(f32[8,512,512]{2,1,0:T(8,128)} %fusion.70, f32[8,512,512]{2,1,0:T(8,128)} %copy-done.1), kind=kOutput, calls=%fused_computation.73 | convolution fusion | flops 12884901888 | bytes 25165824 | tf_op jit(solution)/shard_map/xij,xjk->xik/dot_general | solution.py:14
  622.3 17.2 %fusion.12 = f32[8,512,512]{2,1,0:T(8,128)} fusion(f32[8,512,512]{2,1,0:T(8,128)S(1)} %fusion.71, f32[512,512]{1,0:T(8,128)S(1)} %get-tuple-element.8), kind=kOutput, calls=%fused_computation.22 | convolution fusion | flops 12889096192 | bytes 17825792 | tf_op jit(solution)/shard_map/xij,xjk->xik/dot_general | solution.py:14
  639.5 17.6 %fusion.13 = f32[8,512,512]{2,1,0:T(8,128)} fusion(f32[8,512,512]{2,1,0:T(8,128)} %fusion.11, f32[8,512,512]{2,1,0:T(8,128)S(1)} %fusion.71, f32[512,512]{1,0:T(8,128)S(1)} %get-tuple-element.8), kind=kOutput, calls=%fused_computation.23 | convolution fusion | flops 12889096192 | bytes 26214400 | tf_op jit(solution)/shard_map/xij,xjk->xik/dot_general | solution.py:14
  657.2 22.0 %fusion.72 = f32[8,512,512]{2,1,0:T(8,128)} fusion(f32[8,512,512]{2,1,0:T(8,128)} %fusion.12), kind=kOutput, calls=%fused_computation.74 | convolution fusion | flops 12884901888 | bytes 16777216 | tf_op jit(solution)/shard_map/xij,xjk->xik/dot_general | solution.py:14
  679.2 17.1 %fusion.73 = f32[8,512,512]{2,1,0:T(8,128)} fusion(f32[8,512,512]{2,1,0:T(8,128)} %fusion.72, f32[8,512,512]{2,1,0:T(8,128)S(1)} %fusion.71), kind=kOutput, calls=%fused_computation.75 | convolution fusion | flops 12884901888 | bytes 25165824 | tf_op jit(solution)/shard_map/xij,xjk->xik/dot_general | solution.py:14
  696.3 22.6 %fusion.14 = f32[8,512,512]{2,1,0:T(8,128)} fusion(f32[8,512,512]{2,1,0:T(8,128)} %fusion.73, f32[512,512]{1,0:T(8,128)S(1)} %get-tuple-element.8), kind=kOutput, calls=%fused_computation.24 | convolution fusion | flops 12889096192 | bytes 17825792 | tf_op jit(solution)/shard_map/xij,xjk->xik/dot_general | solution.py:14
  718.9 17.7 %fusion.15 = f32[8,512,512]{2,1,0:T(8,128)} fusion(f32[8,512,512]{2,1,0:T(8,128)} %fusion.13, f32[8,512,512]{2,1,0:T(8,128)S(1)} %copy-done, f32[512,512]{1,0:T(8,128)S(1)} %get-tuple-element.8), kind=kOutput, calls=%fused_computation.25 | convolution fusion | flops 12889096192 | bytes 26214400 | tf_op jit(solution)/shard_map/xij,xjk->xik/dot_general | solution.py:14
  736.6 21.9 %fusion.74 = f32[8,512,512]{2,1,0:T(8,128)} fusion(f32[8,512,512]{2,1,0:T(8,128)} %fusion.14), kind=kOutput, calls=%fused_computation.76 | convolution fusion | flops 12884901888 | bytes 16777216 | tf_op jit(solution)/shard_map/xij,xjk->xik/dot_general | solution.py:14
  758.4 17.0 %fusion.75 = f32[8,512,512]{2,1,0:T(8,128)} fusion(f32[8,512,512]{2,1,0:T(8,128)} %fusion.74, f32[8,512,512]{2,1,0:T(8,128)S(1)} %copy-done), kind=kOutput, calls=%fused_computation.77 | convolution fusion | flops 12884901888 | bytes 25165824 | tf_op jit(solution)/shard_map/xij,xjk->xik/dot_general | solution.py:14
  775.5 19.8 %multiply_convert_fusion = bf16[8,512,512]{2,1,0:T(8,128)(2,1)} fusion(f32[8]{0:T(128)S(1)} %get-tuple-element.6, f32[8,512,512]{2,1,0:T(8,128)} %fusion.15, f32[8,512,512]{2,1,0:T(8,128)} %fusion.75, f32[512,512]{1,0:T(8,128)S(1)} %get-tuple-element.8), kind=kOutput, calls=%fused_computation.5 | convolution fusion | flops 12893290496 | bytes 22020128 | tf_op jit(solution)/shard_map/xij,xjk->xik/dot_general | solution.py:14
  806.8 87.6 %all-gather.2.cloned.1.call-done = bf16[4096,1024]{1,0:T(8,128)(2,1)} async-done(((bf16[1024,1024]{1,0:T(8,128)(2,1)}), bf16[4096,1024]{1,0:T(8,128)(2,1)}) %all-gather.2.cloned.1.call-update) | async-done | bytes 8388624 | tf_op jit(solution)/shard_map/all_gather | solution.py:86
  894.5 189.6 %all_to_all.39 = bf16[8,512,1024]{2,1,0:T(8,128)(2,1)} all-to-all(bf16[8,512,1024]{2,1,0:T(8,128)(2,1)} %bitcast.85), channel_id=1, replica_groups=mesh['rep'=4,'tp'=8] {'tp'}, dimensions={0} | all-to-all | bytes 16777216 | tf_op jit(solution)/shard_map/all_to_all | solution.py:87
  (35 shorter events, 104.8 us)
Async XLA Ops:
  6.5 308.3 %reduce-scatter.5.cloned.1.call-start = ((), (), s32[]{:S(2)}) async-start(), calls=%async_computation.5 | async-start | bytes 10485760 | tf_op jit(solution)/shard_map/reduce_scatter | solution.py:73
  228.8 242.8 %reduce-scatter.3.cloned.1.call-start = ((), (), s32[]{:S(2)}) async-start(), calls=%async_computation.4 | async-start | bytes 20971520 | tf_op jit(solution)/shard_map/reduce_scatter | solution.py:70
  282.2 612.3 %all-gather.2.cloned.1.call-start = ((), (), s32[]{:S(2)}) async-start(), calls=%async_computation.6 | async-start | bytes 10485760 | tf_op jit(solution)/shard_map/all_gather | solution.py:86
  497.3 16.4 %copy-start.2 = (bf16[8,512,512]{2,1,0:T(8,128)(2,1)S(1)}, bf16[8,512,512]{2,1,0:T(8,128)(2,1)}, u32[]{:S(2)}) copy-start(bf16[8,512,512]{2,1,0:T(8,128)(2,1)} %reduce-scatter.3.cloned.1.call-done) | copy-start | bytes 12582916
  497.3 16.4 %copy-start.3 = (f32[512,512]{1,0:T(8,128)S(1)}, f32[512,512]{1,0:T(8,128)}, u32[]{:S(2)}) copy-start(f32[512,512]{1,0:T(8,128)} %get-tuple-element.7) | copy-start | bytes 3145732
  531.9 34.5 %copy-start.1 = (f32[8,512,512]{2,1,0:T(8,128)}, f32[8,512,512]{2,1,0:T(8,128)S(1)}, u32[]{:S(2)}) copy-start(f32[8,512,512]{2,1,0:T(8,128)S(1)} %fusion.65) | copy-start | bytes 25165828
  531.9 17.3 %copy-start.5 = (f32[512,512]{1,0:T(8,128)S(1)}, f32[512,512]{1,0:T(8,128)}, u32[]{:S(2)}) copy-start(f32[512,512]{1,0:T(8,128)} %fusion.54) | copy-start | bytes 3145732
  696.3 22.6 %copy-start = (f32[8,512,512]{2,1,0:T(8,128)S(1)}, f32[8,512,512]{2,1,0:T(8,128)}, u32[]{:S(2)}) copy-start(f32[8,512,512]{2,1,0:T(8,128)} %fusion.73) | copy-start | bytes 25165828
  775.5 19.8 %copy-start.4 = (bf16[2,512,2,512]{3,2,1,0:T(2,128)(2,1)S(1)}, bf16[2,512,2,512]{3,2,1,0:T(2,128)(2,1)}, u32[]{:S(2)}) copy-start(bf16[2,512,2,512]{3,2,1,0:T(2,128)(2,1)} %reshape.47) | copy-start | bytes 6291460
Sparse Core Ops, SparseCore 0:
  229.0 85.8 reduce-scatter.4
  317.9 153.7 reduce-scatter.2
  807.0 87.4 all-gather.1
where the time goes:
time: 1120 us; the launch traced here: 1110 us
  blocking collectives  380 us (34%)
  matrix products  351 us (31%)
  waiting for transfers between devices  269 us (24%)
  local copies, waits for them, and re-layouts  81.9 us (7%)
  other arithmetic  16.9 us (2%)
  between operations  14.3 us (1%)
    dot_general x17, matrix products, multiply(): jnp.einsum('xij,xjk->xik', left_side, right_side, precision=lax.Precision...  319 us
    all_to_all x1, blocking collectives, local(): lax.all_to_all(picked, 'tp', split_axis=1, concat_axis=0, tiled=True)  190 us
    all_to_all x1, blocking collectives, local(): lax.all_to_all(gathered, 'tp', split_axis=0, concat_axis=1, tiled=True)  190 us
    reduce_scatter x1, waiting for transfers between devices, local(): lax.psum_scatter(gram_stack.astype(jnp.bfloat16), 'rep', scatter_dimensio...  152 us
    all_gather x1, waiting for transfers between devices, local(): gathered = lax.all_gather(to_strip(local_tiles), 'rep', axis=0, tiled=True)  87.6 us
    reduce_scatter x1, waiting for transfers between devices, local(): lax.psum_scatter(column_strip.astype(jnp.float32).astype(jnp.bfloat16), '...  29.8 us
    all_to_all x2, local copies, waits for them, and re-layouts, local(): lax.all_to_all(gathered, 'tp', split_axis=0, concat_axis=1, tiled=True)  23.3 us
  transfers between devices with their start and end apart: 3, of which 3 were waited for; matrix products, arithmetic and copies ran while one was open for 5% of the time, Pallas kernels for 0%

commit v1 on v0

v1 whole, which is shorter than its diff:
```python
import jax
import jax.numpy as jnp
from jax import lax
from jax.sharding import PartitionSpec as P

TILE = 512
NS_ITERS = 5


damping = 0.001


def bf(values):
    return values.astype(jnp.bfloat16)


def multiply(left_side, right_side):
    return jnp.einsum(
        "xij,xjk->xik", bf(left_side), bf(right_side), preferred_element_type=jnp.float32
    )


def inverse_roots(stat_stack):
    identity = jnp.eye(TILE, dtype=jnp.float32)
    frob_norm = jnp.sqrt(jnp.sum(stat_stack * stat_stack, axis=(1, 2), keepdims=True))
    quarter = stat_stack * (0.25 / frob_norm)
    missing = quarter
    scale = 1.25
    square_scale = 1.25 * 1.25
    for _ in range(NS_ITERS - 1):
        square = 2.5 * quarter - multiply(quarter, quarter)
        fourth = 2.0 * square_scale * square - multiply(square, square)
        quarter = square_scale * square_scale * quarter - multiply(fourth, quarter)
        missing = 1.25 * missing + scale * quarter - multiply(missing, quarter)
        scale = scale * 1.25
    return bf((scale * identity - missing) * frob_norm ** (-0.25))


def to_grid(strip_rows, tile):
    return strip_rows.reshape(
        strip_rows.shape[0] // tile, tile, strip_rows.shape[1] // tile, tile
    ).transpose(0, 2, 1, 3)


def to_strip(tile_grid):
    grid_rows, grid_cols, tile, _ = tile_grid.shape
    return tile_grid.transpose(0, 2, 1, 3).reshape(grid_rows * tile, grid_cols * tile)


def precondition(root_grid, mean_tiles):
    half_product = bf(jnp.einsum(
        "abij,abjk->abik", root_grid[:, :, 0], mean_tiles, preferred_element_type=jnp.float32
    ))
    return bf(jnp.einsum(
        "abij,abjk->abik", half_product, root_grid[:, :, 1], preferred_element_type=jnp.float32
    ))


def by_strips(picked, replicas):
    column_strip = lax.all_to_all(picked, "tp", split_axis=1, concat_axis=0, tiled=True)
    grid_rows = column_strip.shape[0] // TILE
    grid_cols = column_strip.shape[1] // TILE
    own_rows = grid_rows // replicas
    tile_set = to_grid(column_strip, TILE)
    left_gram = jnp.einsum(
        "abik,abjk->abij", tile_set, tile_set, preferred_element_type=jnp.float32
    )
    right_gram = jnp.einsum(
        "abki,abkj->abij", tile_set, tile_set, preferred_element_type=jnp.float32
    )
    gram_stack = jnp.stack([left_gram, right_gram], axis=2).reshape(
        grid_rows * grid_cols * 2, TILE, TILE
    )
    gram_sums, strip_sum = (
        lax.psum_scatter(
            bf(gram_stack), "rep", scatter_dimension=0, tiled=True
        ).astype(jnp.float32),
        lax.psum_scatter(
            column_strip, "rep", scatter_dimension=0, tiled=True
        ).astype(jnp.float32),
    )
    mean_part = bf(strip_sum / replicas)
    identity = jnp.eye(TILE, dtype=jnp.float32)
    root_stack = inverse_roots(gram_sums / (replicas * TILE) + damping * identity)
    local_tiles = precondition(
        root_stack.reshape(own_rows, grid_cols, 2, TILE, TILE), to_grid(mean_part, TILE)
    )
    gathered = lax.all_gather(to_strip(local_tiles), "rep", axis=0, tiled=True)
    return lax.all_to_all(gathered, "tp", split_axis=0, concat_axis=1, tiled=True)


def by_rows(picked, replicas):
    rows, cols = picked.shape
    own = cols // replicas
    blocks = picked.reshape(rows, replicas, own).transpose(1, 0, 2)
    blocks = lax.all_to_all(blocks, "rep", split_axis=0, concat_axis=0, tiled=True)
    tile_set = blocks.reshape(
        replicas, rows // TILE, TILE, own // TILE, TILE
    ).transpose(1, 3, 0, 2, 4)
    left_gram = jnp.einsum(
        "abrik,abrjk->abij", tile_set, tile_set, preferred_element_type=jnp.float32
    )
    right_gram = jnp.einsum(
        "abrki,abrkj->abij", tile_set, tile_set, preferred_element_type=jnp.float32
    )
    mean_tiles = bf(jnp.sum(tile_set.astype(jnp.float32), axis=2) / replicas)
    identity = jnp.eye(TILE, dtype=jnp.float32)
    stats = jnp.stack([left_gram, right_gram], axis=2) / (replicas * TILE) + damping * identity
    roots = inverse_roots(stats.reshape(-1, TILE, TILE)).reshape(stats.shape)
    strip = to_strip(precondition(roots, mean_tiles))
    return lax.all_gather(strip, "rep", axis=1, tiled=True)


def local(deltas, staleness):
    replicas = lax.axis_size("rep")
    picked = lax.dynamic_index_in_dim(deltas[0], staleness[0], 0, keepdims=False)
    rows, cols = picked.shape
    if rows % TILE == 0 and cols % (replicas * TILE) == 0:
        return by_rows(picked, replicas)
    return by_strips(picked, replicas)


def solution(mesh):
    return jax.shard_map(
        local,
        mesh=mesh,
        in_specs=(P("rep", None, "tp", None), P("rep")),
        out_specs=P("tp", None),
        check_vma=False,
    )
```

time: 1120 us -> 518 us (0.46)
  blocking collectives: 380 us -> 0 us
  matrix products: 351 us -> 240 us
  waiting for transfers between devices: 269 us -> 182 us
  local copies, waits for them, and re-layouts: 81.9 us -> 49.9 us
    all_to_all x2 -> x0, blocking collectives: 380 us -> none  [the longest x1 190 us: local(): lax.all_to_all(picked, 'tp', split_axis=1, concat_axis=0, tiled=True)]
    reduce_scatter x2 -> x0, waiting for transfers between devices: 182 us -> none  [the longest x1 152 us: local(): lax.psum_scatter(gram_stack.astype(jnp.bfloat16), 'rep', scatter_dimensio...]
    dot_general x19 -> x14, matrix products: 345 us -> 234 us  [the longest x12 212 us: multiply(): jnp.einsum('xij,xjk->xik', bf(left_side), bf(right_side), preferred_eleme...]
    all_to_all x0 -> x1, waiting for transfers between devices: none -> 93.6 us  [by_rows(): lax.all_to_all(blocks, 'rep', split_axis=0, concat_axis=0, tiled=True)]
    all_to_all x3 -> x0, local copies, waits for them, and re-layouts: 34.8 us -> none  [the longest x2 23.3 us: local(): lax.all_to_all(gathered, 'tp', split_axis=0, concat_axis=1, tiled=True)]
  transfers between devices with their start and end apart: 3 -> 2, of which waited for: 3 -> 2; matrix products, arithmetic and copies ran while one was open for 5% -> 0% of each run, Pallas kernels for 0% -> 0%
where the time goes in v1:
time: 518 us; the launch traced here: 509 us
  matrix products  240 us (46%)
  waiting for transfers between devices  182 us (35%)
  local copies, waits for them, and re-layouts  49.9 us (10%)
  other arithmetic  17.5 us (3%)
  between operations  14.6 us (3%)
  starting transfers between devices  5.67 us (1%)
    dot_general x12, matrix products, multiply(): jnp.einsum('xij,xjk->xik', bf(left_side), bf(right_side), preferred_eleme...  212 us
    all_to_all x1, waiting for transfers between devices, by_rows(): lax.all_to_all(blocks, 'rep', split_axis=0, concat_axis=0, tiled=True)  93.6 us
    all_gather x1, waiting for transfers between devices, by_rows(): return lax.all_gather(strip, 'rep', axis=1, tiled=True)  88.2 us
    dynamic_slice x2, local copies, waits for them, and re-layouts, local(): lax.dynamic_index_in_dim(deltas[0], staleness[0], 0, keepdims=False)  19.7 us
    reshape x1, local copies, waits for them, and re-layouts, by_rows(): blocks.reshape(replicas, rows // TILE, TILE, own // TILE, TILE)  13.2 us
    dot_general x1, matrix products, by_rows(): jnp.einsum('abrik,abrjk->abij', tile_set, tile_set, preferred_element_typ...  12.2 us
  transfers between devices with their start and end apart: 2, of which 2 were waited for; matrix products, arithmetic and copies ran while one was open for 0% of the time, Pallas kernels for 0%

profile of v1, /device:TPU:0, one launch (start us, length us, event | category | flops | bytes accessed | tf_op | source)
XLA Modules:
  0.0 509.2 jit_solution(10359477175798300883)
XLA Ops:
  7.2 7.8 %constant_dynamic-slice_fusion = bf16[1,1,512,8192]{3,2,1,0:T(8,128)(2,1)} fusion(bf16[1,3,512,8192]{3,2,1,0:T(8,128)(2,1)} %param.2, s32[]{:T(128)S(6)} %select_n.4), kind=kLoop, calls=%fused_computation.67 | loop fusion | bytes 16777220 | tf_op jit(solution)/shard_map/jit(dynamic_index_in_dim)/dynamic_slice | solution.py:116
  15.0 12.0 %copy.12 = bf16[1,1,512,8192]{2,3,1,0:T(8,128)(2,1)} copy(bf16[1,1,512,8192]{3,2,1,0:T(8,128)(2,1)} %constant_dynamic-slice_fusion) | data formatting | bytes 16777216 | tf_op jit(solution)/shard_map/jit(dynamic_index_in_dim)/dynamic_slice | solution.py:116
  26.9 5.6 %all-to-all-start = ((bf16[4,512,2048]{1,2,0:T(8,128)(2,1)}), bf16[4,512,2048]{1,2,0:T(8,128)(2,1)}, u32[]{:S(2)}, u32[]{:S(2)}) async-start(bf16[4,512,2048]{1,2,0:T(8,128)(2,1)} %bitcast.70), calls=%async_computation | async-start | bytes 16777216 | tf_op jit(solution)/shard_map/all_to_all | solution.py:96
  32.9 93.6 %all-to-all-done = bf16[4,512,2048]{1,2,0:T(8,128)(2,1)} async-done(((bf16[4,512,2048]{1,2,0:T(8,128)(2,1)}), bf16[4,512,2048]{1,2,0:T(8,128)(2,1)}, u32[]{:S(2)}, u32[]{:S(2)}) %all-to-all-start) | async-done | bytes 8388640 | tf_op jit(solution)/shard_map/all_to_all | solution.py:96
  126.4 13.2 %copy.13 = bf16[4,1,512,4,512]{4,2,3,0,1:T(8,128)(2,1)} copy(bf16[4,1,512,4,512]{2,4,3,0,1:T(8,128)(2,1)} %bitcast.3) | data formatting | bytes 16777216 | tf_op jit(solution)/shard_map/reshape | solution.py:97
  139.6 12.2 %fusion.52 = f32[1,4,1,512,512]{4,3,1,2,0:T(8,128)} fusion(bf16[4,1,512,4,512]{4,2,3,0,1:T(8,128)(2,1)} %copy.13), kind=kOutput, calls=%fused_computation.53 | convolution fusion | flops 4294967296 | bytes 12582912 | tf_op jit(solution)/shard_map/abrik,abrjk->abij/dot_general | solution.py:100
  151.9 7.3 %convert_reduce_fusion = f32[4,512,512]{2,1,0:T(8,128)} fusion(bf16[4,1,512,4,512]{4,2,3,0,1:T(8,128)(2,1)} %copy.13), kind=kLoop, calls=%fused_computation | loop fusion | flops 7340032 | bytes 12582912 | tf_op jit(solution)/shard_map/reduce_sum | solution.py:106
  159.2 9.4 %fusion.55 = f32[1,4,1,512,512]{4,3,1,2,0:T(8,128)} fusion(bf16[4,4,512,512]{2,3,0,1:T(8,128)(2,1)} %bitcast.9, bf16[4,1,512,4,512]{4,2,3,0,1:T(8,128)(2,1)S(1)} %copy-done.2), kind=kOutput, calls=%fused_computation.54 | convolution fusion | flops 4294967296 | bytes 20971520 | tf_op jit(solution)/shard_map/abrki,abrkj->abij/dot_general | solution.py:103
  177.9 5.3 %fusion.5 = bf16[8,512,512]{2,1,0:T(8,128)(2,1)S(1)} fusion(f32[1,4,2,512,512]{4,3,2,1,0:T(8,128)} %copy.15, f32[8]{0:T(128)S(1)} %div.25, f32[512,512]{1,0:T(8,128)S(1)} %fusion.65), kind=kLoop, calls=%fused_computation.25 | loop fusion | flops 6291456 | bytes 13631520 | tf_op jit(solution)/shard_map/convert_element_type | solution.py:14
  185.2 6.9 %multiply_subtract_fusion.7 = f32[8,512,512]{2,1,0:T(8,128)} fusion(f32[1,4,2,512,512]{4,3,2,1,0:T(8,128)S(1)} %copy-done, f32[8]{0:T(128)S(1)} %div.25, f32[512,512]{1,0:T(8,128)S(1)} %fusion.65, bf16[8,512,512]{2,1,0:T(8,128)(2,1)S(1)} %fusion.5), kind=kOutput, calls=%fused_computation.22 | convolution fusion | flops 2155872256 | bytes 22020128 | tf_op jit(solution)/shard_map/xij,xjk->xik/dot_general | solution.py:18
  192.1 17.3 %multiply_subtract_fusion.8 = f32[8,512,512]{2,1,0:T(8,128)} fusion(f32[1,4,2,512,512]{4,3,2,1,0:T(8,128)} %copy.15, f32[8]{0:T(128)S(1)} %div.25, f32[512,512]{1,0:T(8,128)S(1)} %fusion.65, bf16[8,512,512]{2,1,0:T(8,128)(2,1)} %copy-done.1, f32[8,512,512]{2,1,0:T(8,128)} %multiply_subtract_fusion.7), kind=kOutput, calls=%fused_computation.23 | convolution fusion | flops 4311744512 | bytes 30408736 | tf_op jit(solution)/shard_map/xij,xjk->xik/dot_general | solution.py:18
  209.4 15.2 %multiply_subtract_fusion = f32[8,512,512]{2,1,0:T(8,128)} fusion(f32[8,512,512]{2,1,0:T(8,128)} %multiply_subtract_fusion.8, f32[1,4,2,512,512]{4,3,2,1,0:T(8,128)} %copy.15, f32[8]{0:T(128)S(1)} %div.25, f32[512,512]{1,0:T(8,128)S(1)} %fusion.65, bf16[8,512,512]{2,1,0:T(8,128)(2,1)} %copy-done.1), kind=kOutput, calls=%fused_computation.8 | convolution fusion | flops 2160066560 | bytes 30408736 | tf_op jit(solution)/shard_map/xij,xjk->xik/dot_general | solution.py:18
  224.6 11.5 %fusion.77 = f32[8,512,512]{2,1,0:T(8,128)} fusion(f32[8,512,512]{2,1,0:T(8,128)} %multiply_subtract_fusion.8), kind=kOutput, calls=%fused_computation.78 | convolution fusion | flops 2149580800 | bytes 16777216 | tf_op jit(solution)/shard_map/xij,xjk->xik/dot_general | solution.py:18
  236.3 28.5 %multiply_subtract_fusion.6 = f32[8,512,512]{2,1,0:T(8,128)} fusion(f32[8,512,512]{2,1,0:T(8,128)} %multiply_subtract_fusion.8, f32[8,512,512]{2,1,0:T(8,128)} %fusion.77), kind=kOutput, calls=%fused_computation.20 | convolution fusion | flops 4318035968 | bytes 25165824 | tf_op jit(solution)/shard_map/xij,xjk->xik/dot_general | solution.py:18
  264.8 11.5 %fusion.73 = f32[8,512,512]{2,1,0:T(8,128)} fusion(f32[8,512,512]{2,1,0:T(8,128)} %multiply_subtract_fusion.6), kind=kOutput, calls=%fused_computation.74 | convolution fusion | flops 2149580800 | bytes 16777216 | tf_op jit(solution)/shard_map/xij,xjk->xik/dot_general | solution.py:18
  276.3 16.3 %add_subtract_fusion.1 = f32[8,512,512]{2,1,0:T(8,128)} fusion(f32[8,512,512]{2,1,0:T(8,128)} %multiply_subtract_fusion.6, f32[8,512,512]{2,1,0:T(8,128)} %multiply_subtract_fusion), kind=kOutput, calls=%fused_computation.17 | convolution fusion | flops 2160066560 | bytes 25165824 | tf_op jit(solution)/shard_map/xij,xjk->xik/dot_general | solution.py:18
  292.6 28.8 %multiply_subtract_fusion.4 = f32[8,512,512]{2,1,0:T(8,128)} fusion(f32[8,512,512]{2,1,0:T(8,128)} %multiply_subtract_fusion.6, f32[8,512,512]{2,1,0:T(8,128)} %fusion.73), kind=kOutput, calls=%fused_computation.16 | convolution fusion | flops 4318035968 | bytes 25165824 | tf_op jit(solution)/shard_map/xij,xjk->xik/dot_general | solution.py:18
  321.4 11.5 %fusion.68 = f32[8,512,512]{2,1,0:T(8,128)} fusion(f32[8,512,512]{2,1,0:T(8,128)} %multiply_subtract_fusion.4), kind=kOutput, calls=%fused_computation.69 | convolution fusion | flops 2149580800 | bytes 16777216 | tf_op jit(solution)/shard_map/xij,xjk->xik/dot_general | solution.py:18
  333.0 26.3 %fusion.9 = f32[8,512,512]{2,1,0:T(8,128)} fusion(f32[8,512,512]{2,1,0:T(8,128)} %fusion.68, f32[8,512,512]{2,1,0:T(8,128)} %multiply_subtract_fusion.4), kind=kOutput, calls=%fused_computation.29 | convolution fusion | flops 4313841664 | bytes 25165824 | tf_op jit(solution)/shard_map/xij,xjk->xik/dot_general | solution.py:18
  359.2 11.5 %fusion.17 = f32[8,512,512]{2,1,0:T(8,128)} fusion(f32[8,512,512]{2,1,0:T(8,128)} %add_subtract_fusion.1, f32[8,512,512]{2,1,0:T(8,128)} %multiply_subtract_fusion.4), kind=kOutput, calls=%fused_computation.36 | convolution fusion | flops 2151677952 | bytes 25165824 | tf_op jit(solution)/shard_map/xij,xjk->xik/dot_general | solution.py:18
  370.8 27.0 %multiply_convert_fusion = bf16[8,512,512]{2,1,0:T(8,128)(2,1)} fusion(f32[8]{0:T(128)S(1)} %pow.12, f32[8,512,512]{2,1,0:T(8,128)} %fusion.9, f32[8,512,512]{2,1,0:T(8,128)} %multiply_subtract_fusion.4, f32[8,512,512]{2,1,0:T(8,128)} %fusion.17, f32[8,512,512]{2,1,0:T(8,128)} %add_subtract_fusion.1, f32[512,512]{1,0:T(8,128)S(1)} %fusion.66), kind=kOutput, calls=%fused_computation.9 | convolution fusion | flops 2191523840 | bytes 38797344 | tf_op jit(solution)/shard_map/xij,xjk->xik/dot_general | solution.py:18
  397.8 5.8 %fusion.62 = bf16[4,512,512]{1,2,0:T(8,128)(2,1)S(1)} fusion(bf16[1,4,2,512,512]{4,3,2,1,0:T(8,128)(2,1)} %bitcast.72, f32[4,512,512]{2,1,0:T(8,128)} %convert_reduce_fusion), kind=kOutput, calls=%fused_computation.61 | convolution fusion | flops 2151677952 | bytes 10485760 | tf_op jit(solution)/shard_map/abij,abjk->abik/dot_general | solution.py:54
  406.0 88.2 %all-gather.2.cloned.1.call-done = bf16[512,8192]{1,0:T(8,128)(2,1)} async-done(((bf16[512,2048]{1,0:T(8,128)(2,1)}), bf16[512,8192]{1,0:T(8,128)(2,1)}) %all-gather.2.cloned.1.call-update) | async-done | bytes 8388624 | tf_op jit(solution)/shard_map/all_gather | solution.py:111
  494.1 7.8 %copy.28 = bf16[512,8192]{1,0:T(8,128)(2,1)} copy(bf16[512,8192]{1,0:T(8,128)(2,1)} %all-gather.2.cloned.1.call-done) | data formatting | bytes 16777216
  (18 shorter events, 14.1 us)
Async XLA Ops:
  26.9 99.5 %all-to-all-start = ((bf16[4,512,2048]{1,2,0:T(8,128)(2,1)}), bf16[4,512,2048]{1,2,0:T(8,128)(2,1)}, u32[]{:S(2)}, u32[]{:S(2)}) async-start(bf16[4,512,2048]{1,2,0:T(8,128)(2,1)} %bitcast.70), calls=%async_computation | async-start | bytes 16777216 | tf_op jit(solution)/shard_map/all_to_all | solution.py:96
  32.6 461.6 %all-gather.2.cloned.1.call-start = ((), (), s32[]{:S(2)}) async-start(), calls=%async_computation.1 | async-start | bytes 10485760 | tf_op jit(solution)/shard_map/all_gather | solution.py:111
  151.9 7.3 %copy-start.2 = (bf16[4,1,512,4,512]{4,2,3,0,1:T(8,128)(2,1)S(1)}, bf16[4,1,512,4,512]{4,2,3,0,1:T(8,128)(2,1)}, u32[]{:S(2)}) copy-start(bf16[4,1,512,4,512]{4,2,3,0,1:T(8,128)(2,1)} %copy.13) | copy-start | bytes 25165828
  177.9 7.3 %copy-start = (f32[1,4,2,512,512]{4,3,2,1,0:T(8,128)S(1)}, f32[1,4,2,512,512]{4,3,2,1,0:T(8,128)}, u32[]{:S(2)}) copy-start(f32[1,4,2,512,512]{4,3,2,1,0:T(8,128)} %copy.15) | copy-start | bytes 25165828
  183.2 1.9 copy-start.1
Sparse Core Ops, SparseCore 0:
  406.1 87.9 all-gather.1

commit v2 on v1

--- a/solution.py
+++ b/solution.py
@@ -1,6 +1,10 @@
+import functools
+
 import jax
 import jax.numpy as jnp
 from jax import lax
+from jax.experimental import pallas as pl
+from jax.experimental.pallas import tpu as pltpu
 from jax.sharding import PartitionSpec as P
 
 TILE = 512
@@ -89,26 +93,232 @@
     return lax.all_to_all(gathered, "tp", split_axis=0, concat_axis=1, tiled=True)
 
 
+BLOCK = 256
+AHEAD = 2
+RELAY = True
+COMPUTE = True
+
+
+def product(left_side, right_side, contract=((1,), (0,))):
+    return lax.dot_general(
+        left_side, right_side, (contract, ((), ())), preferred_element_type=jnp.float32
+    )
+
+
+def tile_root(quarter, square, fourth, missing, norms):
+    blocks = [pl.ds(start, BLOCK) for start in range(0, TILE, BLOCK)]
+
+    def step(_, scale):
+        first = 1.25 * 1.25
+        for side in range(2):
+            for rows in blocks:
+                mine = quarter[side, rows, :]
+                square[side, rows, :] = bf(2.5 * mine - product(mine, quarter[side]))
+        for side in range(2):
+            for rows in blocks:
+                mine = square[side, rows, :]
+                fourth[side, rows, :] = bf(2.0 * first * mine - product(mine, square[side]))
+        for side in range(2):
+            for rows in blocks:
+                mine = quarter[side, rows, :]
+                quarter[side, rows, :] = bf(first * first * mine - product(mine, fourth[side]))
+        for side in range(2):
+            for rows in blocks:
+                mine = missing[side, rows, :]
+                missing[side, rows, :] = bf(
+                    1.25 * mine + scale * quarter[side, rows, :] - product(mine, quarter[side])
+                )
+        return scale * 1.25
+
+    scale = lax.fori_loop(0, NS_ITERS - 1, step, jnp.float32(1.25))
+    for side in range(2):
+        for start, rows in zip(range(0, TILE, BLOCK), blocks):
+            row = lax.broadcasted_iota(jnp.int32, (BLOCK, TILE), 0) + start
+            col = lax.broadcasted_iota(jnp.int32, (BLOCK, TILE), 1)
+            full = jnp.where(row == col, scale, 0.0) - missing[side, rows, :]
+            square[side, rows, :] = bf(full * norms[side])
+
+
+def tile_update(parts, out_ref, count, gram, quarter, square, fourth, missing):
+    starts = range(0, TILE, BLOCK)
+    norms = []
+    for side in range(2):
+        total = jnp.zeros((1, 1), jnp.float32)
+        for start in starts:
+            rows = pl.ds(start, BLOCK)
+            acc = None
+            for r in range(count):
+                if side == 0:
+                    term = product(parts[r, rows, :], parts[r], ((1,), (1,)))
+                else:
+                    term = product(parts[r, :, rows], parts[r], ((0,), (0,)))
+                acc = term if acc is None else acc + term
+            row = lax.broadcasted_iota(jnp.int32, (BLOCK, TILE), 0) + start
+            col = lax.broadcasted_iota(jnp.int32, (BLOCK, TILE), 1)
+            acc = acc * (1.0 / (count * TILE)) + jnp.where(row == col, damping, 0.0)
+            gram[side, rows, :] = acc
+            total = total + jnp.sum(
+                jnp.sum(acc * acc, axis=0, keepdims=True), axis=1, keepdims=True
+            )
+        for start in starts:
+            rows = pl.ds(start, BLOCK)
+            value = bf(gram[side, rows, :] * (0.25 * lax.rsqrt(total)))
+            quarter[side, rows, :] = value
+            missing[side, rows, :] = value
+        norms.append(lax.rsqrt(jnp.sqrt(jnp.sqrt(total))))
+    tile_root(quarter, square, fourth, missing, norms)
+    for start in starts:
+        rows = pl.ds(start, BLOCK)
+        total = parts[0, rows, :].astype(jnp.float32)
+        for r in range(1, count):
+            total = total + parts[r, rows, :].astype(jnp.float32)
+        fourth[0, rows, :] = bf(total * (1.0 / count))
+    for start in starts:
+        rows = pl.ds(start, BLOCK)
+        half = bf(product(square[0, rows, :], fourth[0]))
+        out_ref[rows, :] = bf(product(half, square[1]))
+
+
+def exchange_kernel(
+    count, picked, out_ref, parts, tiles, gram, quarter, square, fourth,
+    missing, in_send, in_recv, in_copy, out_send, out_recv, out_copy, hop_send, hop_recv,
+):
+    me = lax.axis_index("rep")
+    rows, cols = out_ref.shape
+    across = cols // TILE // count
+    own = rows // TILE * across
+    relay = RELAY and count == 4
+    mid = TILE // 2
+
+    def peer(k):
+        return me ^ k if count & (count - 1) == 0 else lax.rem(me + k, count)
+
+    def source(k):
+        return me ^ k if count & (count - 1) == 0 else lax.rem(me + count - k, count)
+
+    def place(ref, owner, t, start=0, size=TILE):
+        top = pl.multiple_of(t // across * TILE + start, size)
+        left = pl.multiple_of((owner * across + lax.rem(t, across)) * TILE, TILE)
+        return ref.at[pl.ds(top, size), pl.ds(left, TILE)]
+
+    def inward(t, k):
+        to = peer(k)
+        return pltpu.make_async_remote_copy(
+            src_ref=place(picked, to, t), dst_ref=parts.at[t, me],
+            send_sem=in_send.at[t, k], recv_sem=in_recv.at[t, k],
+            device_id={"rep": to}, device_id_type=pl.DeviceIdType.MESH,
+        )
+
+    def inward_own(t):
+        return pltpu.make_async_copy(place(picked, me, t), parts.at[t, me], in_copy.at[t])
+
+    def outward(t, k):
+        to = peer(k)
+        return pltpu.make_async_remote_copy(
+            src_ref=tiles.at[t], dst_ref=place(out_ref, me, t),
+            send_sem=out_send.at[t, k], recv_sem=out_recv.at[t, k],
+            device_id={"rep": to}, device_id_type=pl.DeviceIdType.MESH,
+        )
+
+    def outward_own(t):
+        return pltpu.make_async_copy(tiles.at[t], place(out_ref, me, t), out_copy.at[t])
+
+    def hop(t, k):
+        half = place(out_ref, me ^ k, t, (k - 1) * mid, mid)
+        return pltpu.make_async_remote_copy(
+            src_ref=half, dst_ref=half,
+            send_sem=hop_send.at[t, k], recv_sem=hop_recv.at[t, k],
+            device_id={"rep": me ^ (3 - k)}, device_id_type=pl.DeviceIdType.MESH,
+        )
+
+    direct = range(1, 3) if relay else range(1, count)
+
+    def send_in(t):
+        for k in range(1, count):
+            inward(t, k).start()
+        inward_own(t).start()
+
+    def forward(t):
+        for k in (1, 2):
+            outward(t, k).wait_recv()
+            hop(t, k).start()
+
+    barrier = pltpu.get_barrier_semaphore()
+    for k in range(1, count):
+        pl.semaphore_signal(
+            barrier, inc=1, device_id={"rep": peer(k)}, device_id_type=pl.DeviceIdType.MESH
+        )
+    pl.semaphore_wait(barrier, count - 1)
+
+    for t in range(min(AHEAD, own)):
+        send_in(t)
+
+    @pl.loop(0, own)
+    def _(t):
+        inward_own(t).wait()
+        for k in range(1, count):
+            inward(t, k).wait()
+
+        @pl.when(t + AHEAD < own)
+        def _():
+            send_in(t + AHEAD)
+
+        if COMPUTE:
+            tile_update(
+                parts.at[t], tiles.at[t], count, gram, quarter, square, fourth, missing
+            )
+        for k in direct:
+            outward(t, k).start()
+        outward_own(t).start()
+        if relay:
+
+            @pl.when(t > 0)
+            def _():
+                forward(t - 1)
+
+    if relay:
+        forward(own - 1)
+
+    @pl.loop(0, own)
+    def _(t):
+        outward_own(t).wait()
+        for k in direct:
+            outward(t, k).wait_send()
+            if not relay:
+                outward(t, k).wait_recv()
+        if relay:
+            for k in (1, 2):
+                hop(t, k).wait()
+
+
 def by_rows(picked, replicas):
     rows, cols = picked.shape
-    own = cols // replicas
-    blocks = picked.reshape(rows, replicas, own).transpose(1, 0, 2)
-    blocks = lax.all_to_all(blocks, "rep", split_axis=0, concat_axis=0, tiled=True)
-    tile_set = blocks.reshape(
-        replicas, rows // TILE, TILE, own // TILE, TILE
-    ).transpose(1, 3, 0, 2, 4)
-    left_gram = jnp.einsum(
-        "abrik,abrjk->abij", tile_set, tile_set, preferred_element_type=jnp.float32
-    )
-    right_gram = jnp.einsum(
-        "abrki,abrkj->abij", tile_set, tile_set, preferred_element_type=jnp.float32
-    )
-    mean_tiles = bf(jnp.sum(tile_set.astype(jnp.float32), axis=2) / replicas)
-    identity = jnp.eye(TILE, dtype=jnp.float32)
-    stats = jnp.stack([left_gram, right_gram], axis=2) / (replicas * TILE) + damping * identity
-    roots = inverse_roots(stats.reshape(-1, TILE, TILE)).reshape(stats.shape)
-    strip = to_strip(precondition(roots, mean_tiles))
-    return lax.all_gather(strip, "rep", axis=1, tiled=True)
+    own = (rows // TILE) * (cols // TILE // replicas)
+    square = pltpu.VMEM((2, TILE, TILE), jnp.bfloat16)
+    pairs = pltpu.SemaphoreType.DMA((own, replicas))
+    single = pltpu.SemaphoreType.DMA((own,))
+    flops = own * (2 * replicas + 34) * 2 * TILE**3
+    return pl.pallas_call(
+        functools.partial(exchange_kernel, replicas),
+        out_shape=jax.ShapeDtypeStruct((rows, cols), jnp.bfloat16),
+        in_specs=[
+            pl.BlockSpec(memory_space=pl.ANY),
+        ],
+        out_specs=pl.BlockSpec(memory_space=pl.ANY),
+        scratch_shapes=[
+            pltpu.VMEM((own, replicas, TILE, TILE), jnp.bfloat16),
+            pltpu.VMEM((own, TILE, TILE), jnp.bfloat16),
+            pltpu.VMEM((2, TILE, TILE), jnp.float32),
+            square, square, square, square,
+            pairs, pairs, single, pairs, pairs, single, pairs, pairs,
+        ],
+        compiler_params=pltpu.CompilerParams(
+            collective_id=0, has_side_effects=True, vmem_limit_bytes=60 * 1024 * 1024
+        ),
+        cost_estimate=pl.CostEstimate(
+            flops=flops, bytes_accessed=4 * rows * cols, transcendentals=0
+        ),
+    )(picked)
 
 
 def local(deltas, staleness):

time: 518 us -> 180 us (0.35); the launches traced: 509 us -> 180 us
  matrix products: 240 us -> 0 us
  waiting for transfers between devices: 182 us -> 0 us
  Pallas kernels: 0 us -> 164 us
  local copies, waits for them, and re-layouts: 49.9 us -> 15.5 us
  other arithmetic: 17.5 us -> 0 us
  between operations: 14.6 us -> 0.66 us
  starting transfers between devices: 5.67 us -> 0 us
    dot_general x15 -> x0, matrix products: 240 us -> none  [the longest x12 212 us: multiply(): jnp.einsum('xij,xjk->xik', bf(left_side), bf(right_side), preferred_eleme...]
    pallas_call x0 -> x1, Pallas kernels: none -> 164 us  [by_rows(): pl.pallas_call(functools.partial(exchange_kernel, replicas), out_shape=ja...]
    all_to_all x1 -> x0, waiting for transfers between devices: 93.6 us -> none  [by_rows(): lax.all_to_all(blocks, 'rep', split_axis=0, concat_axis=0, tiled=True)]
    all_gather x1 -> x0, waiting for transfers between devices: 88.2 us -> none  [by_rows(): return lax.all_gather(strip, 'rep', axis=1, tiled=True)]
    dynamic_slice x2 -> x0, local copies, waits for them, and re-layouts: 19.7 us -> none  [local(): lax.dynamic_index_in_dim(deltas[0], staleness[0], 0, keepdims=False)]
    reshape x2 -> x0, local copies, waits for them, and re-layouts: 15.6 us -> none  [the longest x1 13.2 us: by_rows(): blocks.reshape(replicas, rows // TILE, TILE, own // TILE, TILE)]
    squeeze x0 -> x1, local copies, waits for them, and re-layouts: none -> 7.78 us  [local(): lax.dynamic_index_in_dim(deltas[0], staleness[0], 0, keepdims=False)]
    reduce_sum x1 -> x0, other arithmetic: 7.3 us -> none  [by_rows(): mean_tiles = bf(jnp.sum(tile_set.astype(jnp.float32), axis=2) / replicas)]
  transfers between devices with their start and end apart: 2 -> 0, of which waited for: 2 -> 0; matrix products, arithmetic and copies ran while one was open for 0% -> 0% of each run, Pallas kernels for 0% -> 0%
where the time goes in v2:
time: 180 us
  Pallas kernels  164 us (91%)
  local copies, waits for them, and re-layouts  15.5 us (9%)
    pallas_call x1, Pallas kernels, by_rows(): pl.pallas_call(functools.partial(exchange_kernel, replicas), out_shape=ja...  164 us
    squeeze x1, local copies, waits for them, and re-layouts, local(): lax.dynamic_index_in_dim(deltas[0], staleness[0], 0, keepdims=False)  7.78 us
    unnamed x1, local copies, waits for them, and re-layouts  7.77 us

profile of v2, /device:TPU:0, one launch (start us, length us, event | category | flops | bytes accessed | tf_op | source)
XLA Modules:
  0.0 179.8 jit_solution(6453204820503320987)
XLA Ops:
  0.7 7.8 %dynamic-slice_bitcast_fusion.picked = bf16[512,8192]{1,0:T(8,128)(2,1)} fusion(bf16[1,3,512,8192]{3,2,1,0:T(8,128)(2,1)} %param.2, s32[]{:T(128)S(6)} %select_n.4), kind=kLoop, calls=%fused_computation | loop fusion | bytes 16777220 | tf_op jit(solution)/shard_map/jit(dynamic_index_in_dim)/squeeze | solution.py:326
  8.4 163.6 %shard_map.28 = bf16[512,8192]{1,0:T(8,128)(2,1)} custom-call(bf16[512,8192]{1,0:T(8,128)(2,1)} %dynamic-slice_bitcast_fusion.picked), custom_call_target="tpu_custom_call" | custom-call | flops 45097156608 | bytes 16777216 | tf_op jit(solution)/shard_map/pallas_call | solution.py:301
  172.0 7.8 %copy.5 = bf16[512,8192]{1,0:T(8,128)(2,1)} copy(bf16[512,8192]{1,0:T(8,128)(2,1)} %shard_map.28) | data formatting | bytes 16777216
